TPU v7x, 32 devices: a whole 2x2x4 slice. The times are simulated.
32 devices in a mesh: lat: 8 (over z, y), lon: 4 (over x, core).
Axes of the slice: x: 2, y: 2, z: 4, core: 2. Of those that a mesh axis runs over, the one named last changes fastest.
Arguments:
- pair_table: int32 [640], replicated, may hold values from 0 to 639, each once
- spectral: bfloat16 [640, 384, 1408], P('lat', 'lon'), may hold values from -0.071777344 to 0.071777344
- lat_basis: bfloat16 [640, 32, 1408], P('lat'), may hold values from -0.15625 to 0.15625
- in_weight: bfloat16 [192, 512], replicated, may hold values from -0.4375 to 0.4375
- in_bias: float32 [512], replicated, may hold values from -3 to 3
- out_weight: bfloat16 [512, 192], replicated, may hold values from -0.25 to 0.25
- out_bias: float32 [192], replicated, may hold values from -3 to 3
- cotangent: bfloat16 [64, 192, 2560], P('lat', None, 'lon'), may hold values from -0.08984375 to 0.08984375
Outputs:
- tendency: bfloat16 [64, 192, 2560], P('lat', None, 'lon')
- spectral_grad: bfloat16 [640, 384, 1408], P('lat', 'lon')
- in_weight_grad: float32 [192, 512], replicated
- in_bias_grad: float32 [512], replicated
- out_weight_grad: float32 [512, 192], replicated
- out_bias_grad: float32 [192], replicated
Inputs may be any that keep to these rules, and one draw needn't show every extreme that they name: `pair_table`: each pair number appears exactly once.
All inputs are finite; a program needn't handle non-finite values.
Results may differ from a plain program's by a relative error of at most 0.015.
Values may be sent and summed in bfloat16 or wider, within the bound.
No kernel may reach another device: no remote copies, remote signals or barrier semaphores. Data moves between devices by JAX's collectives and lax.ppermute only.
A program may use at most 256 MiB of HBM per device.

v0:
```python
import math
import jax
import jax.numpy as jnp
from jax import lax
from jax.sharding import PartitionSpec as P

TRUNC = 1279


def pair_masks(pair_ids, length):
    first_len = TRUNC + 1 - pair_ids
    position = jnp.arange(length, dtype=jnp.int32)[None, :]
    lower_part = position < first_len[:, None]
    upper_part = jnp.logical_and(position >= first_len[:, None], position < TRUNC + 2)
    offset = jnp.where(lower_part, position, position - first_len[:, None])
    parity = jnp.where(offset % 2 == 0, 1.0, -1.0).astype(jnp.float32)
    return (lower_part, upper_part, parity, first_len)


def wave_numbers(pair_ids):
    both = jnp.stack([pair_ids, TRUNC - pair_ids], axis=1)
    return both.reshape(-1)


def fourier_table(numbers, lon_total):
    step = 128 if lon_total % 128 == 0 else 1
    coarse = jnp.arange(lon_total // step, dtype=jnp.int32) * step
    fine = jnp.arange(step, dtype=jnp.int32)
    scale = 2.0 * math.pi / lon_total

    def angles(offsets):
        phase = numbers[:, None] * offsets[None, :] % lon_total
        angle = phase.astype(jnp.float32) * scale
        return (jnp.cos(angle), jnp.sin(angle))

    cos_a, sin_a = angles(coarse)
    cos_b, sin_b = angles(fine)
    cos_t = cos_a[:, :, None] * cos_b[:, None, :] - sin_a[:, :, None] * sin_b[:, None, :]
    sin_t = sin_a[:, :, None] * cos_b[:, None, :] + cos_a[:, :, None] * sin_b[:, None, :]
    count = numbers.shape[0]
    factor = jnp.where(numbers == 0, 1.0, 2.0).astype(jnp.float32)[:, None]
    return jnp.stack(
        [factor * cos_t.reshape(count, lon_total), -factor * sin_t.reshape(count, lon_total)],
        axis=1,
    ).astype(jnp.bfloat16)


def per_device(
    pair_table, spectral, lat_basis, in_weight, in_bias, out_weight, out_bias, cotangent
):
    pair_dev = spectral.shape[0]
    width_local = spectral.shape[1]
    lat_half = lat_basis.shape[1]
    band_rows = cotangent.shape[0]
    block_cols = cotangent.shape[2]
    lon_total = block_cols * lax.axis_size("lon")
    first_row = lax.axis_index("lat") * pair_dev
    local_ids = lax.dynamic_slice_in_dim(pair_table, first_row, pair_dev)
    lower_part, upper_part, parity, first_len = pair_masks(local_ids, spectral.shape[2])
    rows = jnp.concatenate([lat_basis, lat_basis * parity[:, None, :].astype(jnp.bfloat16)], axis=1)
    zero = jnp.zeros_like(rows)
    basis = jnp.stack(
        [
            jnp.where(lower_part[:, None, :], rows, zero),
            jnp.where(upper_part[:, None, :], rows, zero),
        ],
        axis=1,
    )
    lat_window = 2 * lat_half
    raw_waves = jnp.einsum(
        "pqlj,pkj->pqlk", basis, spectral, preferred_element_type=jnp.float32
    ).astype(jnp.bfloat16)
    waves = jnp.concatenate(
        [raw_waves[:, :, :lat_half], jnp.flip(raw_waves[:, :, lat_half:], axis=2)], axis=2
    )
    flat_waves = waves.reshape(2 * pair_dev, lat_window * width_local)
    band_waves = lax.all_to_all(flat_waves, "lat", split_axis=1, concat_axis=0, tiled=True)
    wave_count = band_waves.shape[0]
    coeff_grid = band_waves.reshape(wave_count, band_rows, width_local // 2, 2)
    numbers = wave_numbers(pair_table)
    full_table = fourier_table(numbers, lon_total)
    all_columns = jnp.einsum(
        "glkc,gcn->lkn", coeff_grid, full_table, preferred_element_type=jnp.float32
    ).astype(jnp.bfloat16)
    grid = lax.all_to_all(all_columns, "lon", split_axis=2, concat_axis=1, tiled=True)
    pre_act = (
        jnp.einsum("lkc,kh->lch", grid, in_weight, preferred_element_type=jnp.float32) + in_bias
    )
    activated, gelu_back = jax.vjp(jax.nn.gelu, pre_act)
    hidden = activated.astype(jnp.bfloat16)
    tendency = (
        jnp.einsum("lch,hk->lkc", hidden, out_weight, preferred_element_type=jnp.float32)
        + out_bias[None, :, None]
    ).astype(jnp.bfloat16)
    out_weight_part = jnp.einsum(
        "lch,lkc->kh", hidden, cotangent, preferred_element_type=jnp.float32
    )
    out_bias_part = jnp.sum(cotangent.astype(jnp.float32), axis=(0, 2))
    hidden_grad = jnp.einsum(
        "lkc,hk->lch", cotangent, out_weight, preferred_element_type=jnp.float32
    )
    pre_grad = gelu_back(hidden_grad)[0].astype(jnp.bfloat16)
    in_weight_part = jnp.einsum("lkc,lch->kh", grid, pre_grad, preferred_element_type=jnp.float32)
    in_bias_part = jnp.sum(pre_grad.astype(jnp.float32), axis=(0, 1))
    grid_grad = jnp.einsum(
        "lch,kh->lkc", pre_grad, in_weight, preferred_element_type=jnp.float32
    ).astype(jnp.bfloat16)
    channels, hid = in_weight.shape
    width = max(hid, channels)

    def widen(v):
        return jnp.pad(v, ((0, 0), (0, width - v.shape[1])))

    stacked = jnp.concatenate(
        [
            widen(in_weight_part),
            widen(out_weight_part),
            widen(in_bias_part[None, :]),
            widen(out_bias_part[None, :]),
        ],
        axis=0,
    )
    summed = lax.psum(stacked, ("lat", "lon"))
    in_weight_grad = summed[:channels, :hid]
    out_weight_grad = summed[channels : 2 * channels, :hid].T
    in_bias_grad = summed[2 * channels, :hid]
    out_bias_grad = summed[2 * channels + 1, :channels]
    level_rows = lax.all_to_all(grid_grad, "lon", split_axis=1, concat_axis=2, tiled=True)
    wave_grad = jnp.einsum(
        "gcn,lkn->glkc", full_table, level_rows, preferred_element_type=jnp.float32
    ).astype(jnp.bfloat16)
    flat_grad = wave_grad.reshape(wave_count, band_rows * width_local)
    pair_grad = lax.all_to_all(flat_grad, "lat", split_axis=0, concat_axis=1, tiled=True)
    pair_grad = pair_grad.reshape(pair_dev, 2, lat_window, width_local)
    pair_grad = jnp.concatenate(
        [pair_grad[:, :, :lat_half], jnp.flip(pair_grad[:, :, lat_half:], axis=2)], axis=2
    )
    spectral_grad = jnp.einsum(
        "pqlk,pqlj->pkj", pair_grad, basis, preferred_element_type=jnp.float32
    ).astype(jnp.bfloat16)
    return (tendency, spectral_grad, in_weight_grad, in_bias_grad, out_weight_grad, out_bias_grad)


def solution(mesh):
    placed = (
        P(),
        P("lat", "lon", None),
        P("lat", None, None),
        P(),
        P(),
        P(),
        P(),
        P("lat", None, "lon"),
    )
    return jax.shard_map(
        per_device,
        mesh=mesh,
        in_specs=placed,
        out_specs=(P("lat", None, "lon"), P("lat", "lon", None), P(), P(), P(), P()),
        check_vma=False,
    )
```

profile of v0, /device:TPU:1, one launch (start us, length us, event | category | flops | bytes accessed | tf_op | source)
XLA Modules:
  0.0 477.1 jit_solution(11046358141665475062)
XLA Ops:
  8.6 7.1 %multiply_bitcast_fusion = bf16[80,1,32,1408]{3,2,1,0:T(8,128)(2,1)} fusion(bf16[80,32,1408]{2,1,0:T(8,128)(2,1)} %param.10, bf16[80,1408]{1,0:T(8,128)(2,1)S(1)} %select_convert_fusion), kind=kLoop, calls=%fused_computation.25 | loop fusion | flops 3604480 | bytes 14643200 | tf_op jit(solution)/shard_map/concatenate | solution.py:60
  15.7 14.2 %broadcast_select_fusion.1 = (bf16[80,1,64,1408]{3,2,1,0:T(8,128)(2,1)}, bf16[80,1,64,1408]{3,2,1,0:T(8,128)(2,1)}) fusion(pred[80,1408]{1,0:T(8,128)(4,1)S(1)} %get-tuple-element.22, bf16[80,1,32,1408]{3,2,1,0:T(8,128)(2,1)} %multiply_bitcast_fusion, bf16[80,1,32,1408]{3,2,1,0:T(8,128)(2,1)S(1)} %bitcast.97, pred[80,1408]{1,0:T(8,128)(4,1)S(1)} %get-tuple-element.23), kind=kLoop, calls=%fused_computation.8 | loop fusion | flops 43253760 | bytes 43479040 | tf_op jit(solution)/shard_map/jit(_where)/select_n | solution.py:64
  29.8 20.0 %fusion.18 = bf16[80,2,64,96]{3,2,1,0:T(8,128)(2,1)} fusion(bf16[80,96,1408]{2,1,0:T(8,128)(2,1)} %param.9, bf16[80,1,64,1408]{3,2,1,0:T(8,128)(2,1)} %get-tuple-element.7, bf16[80,1,64,1408]{3,2,1,0:T(8,128)(2,1)} %get-tuple-element.6), kind=kOutput, calls=%fused_computation.36 | convolution fusion | flops 2783641600 | bytes 52428800 | tf_op jit(solution)/shard_map/pqlj,pkj->pqlk/dot_general | solution.py:70
  49.8 3.4 fusion.52
  58.3 3.1 all_to_all.50
  61.4 3.2 copy.25
  64.6 6.9 %all-to-all-start = ((bf16[160,8,768]{2,0,1:T(8,128)(2,1)}), bf16[160,8,768]{2,0,1:T(8,128)(2,1)S(1)}, u32[]{:S(2)}, u32[]{:S(2)}) async-start(bf16[160,8,768]{2,0,1:T(8,128)(2,1)} %copy.25), calls=%async_computation | async-start | bytes 3932160 | tf_op jit(solution)/shard_map/all_to_all | solution.py:77
  75.9 13.6 %multiply_subtract_fusion = (f32[1280,20,128]{0,2,1:T(8,128)}, f32[1280,20,128]{0,2,1:T(8,128)}) fusion(f32[1280,128]{0,1:T(8,128)S(1)} %get-tuple-element.21, f32[1280,20]{0,1:T(8,128)} %get-tuple-element.17, f32[1280,128]{0,1:T(8,128)S(1)} %get-tuple-element.20, f32[1280,20]{0,1:T(8,128)} %get-tuple-element.16), kind=kLoop, calls=%fused_computation.13 | loop fusion | flops 19660800 | bytes 27729920 | tf_op jit(solution)/shard_map/sub | solution.py:38
  89.6 14.0 %copy.29 = f32[1280,1,2560]{2,0,1:T(8,128)} copy(f32[1280,1,2560]{0,2,1:T(8,128)} %bitcast.94) | data formatting | bytes 26214400 | tf_op jit(solution)/shard_map/add | solution.py:39
  103.6 14.0 %copy.28 = f32[1280,1,2560]{2,0,1:T(8,128)} copy(f32[1280,1,2560]{0,2,1:T(8,128)} %bitcast.93) | data formatting | bytes 26214400 | tf_op jit(solution)/shard_map/sub | solution.py:38
  117.5 13.9 %multiply_convert_fusion = (bf16[1280,1,2560]{2,0,1:T(8,128)(2,1)}, bf16[1280,1,2560]{2,0,1:T(8,128)(2,1)}) fusion(f32[1280,1,2560]{2,0,1:T(8,128)} %copy.29, f32[1280]{0:T(1024)S(1)} %get-tuple-element.19, f32[1280,1,2560]{2,0,1:T(8,128)} %copy.28, f32[1280]{0:T(1024)S(1)} %get-tuple-element.18), kind=kLoop, calls=%fused_computation.10 | loop fusion | flops 13107200 | bytes 39331840 | tf_op jit(solution)/shard_map/convert.1
  132.7 4.1 copy.26
  136.8 5.2 %reshape.454 = bf16[1280,8,48,2]{0,3,2,1:T(2,128)(2,1)} reshape(bf16[8,160,768]{1,0,2:T(8,128)(2,1)S(1)} %copy.26) | data formatting | bytes 3932160 | tf_op jit(solution)/shard_map/reshape | solution.py:79
  142.1 8.9 %fusion.12 = bf16[8,48,2560]{2,1,0:T(8,128)(2,1)S(1)} fusion(bf16[1280,1,2560]{2,0,1:T(8,128)(2,1)} %get-tuple-element.28, bf16[1280,1,2560]{2,0,1:T(8,128)(2,1)} %get-tuple-element.29, bf16[1280,8,48,2]{0,3,2,1:T(2,128)(2,1)} %reshape.454), kind=kOutput, calls=%fused_computation.27 | convolution fusion | flops 5040701440 | bytes 17039360 | tf_op jit(solution)/shard_map/glkc,gcn->lkn/dot_general | solution.py:82
  151.0 5.4 %copy.31 = bf16[8,48,2560]{1,0,2:T(8,128)(2,1)} copy(bf16[8,48,2560]{2,1,0:T(8,128)(2,1)S(1)} %fusion.12) | data formatting | bytes 3932160 | tf_op jit(solution)/shard_map/convert_element_type | solution.py:84
  156.4 8.8 %reshape.467 = bf16[4,2,122880]{2,1,0:T(2,128)(2,1)S(1)} reshape(bf16[2560,8,48]{2,1,0:T(8,128)(2,1)} %bitcast.98) | data formatting | bytes 3932160
  165.3 27.4 %all_to_all.68 = bf16[4,2,122880]{2,1,0:T(2,128)(2,1)} all-to-all(bf16[4,2,122880]{2,1,0:T(2,128)(2,1)S(1)} %reshape.467), channel_id=1, replica_groups=mesh['lat'=8,'lon'=4] {'lon'}, dimensions={0} | all-to-all | bytes 3932160 | tf_op jit(solution)/shard_map/all_to_all | solution.py:85
  192.7 7.1 %reshape.468 = bf16[2560,8,48]{2,1,0:T(8,128)(2,1)} reshape(bf16[4,2,122880]{2,1,0:T(2,128)(2,1)} %all_to_all.68) | data formatting | bytes 3932160
  199.8 5.7 %copy.32 = bf16[8,48,4,640]{3,1,2,0:T(8,128)(2,1)S(1)} copy(bf16[8,48,4,640]{1,0,3,2:T(8,128)(2,1)} %bitcast.99) | data formatting | bytes 3932160 | tf_op jit(solution)/shard_map/all_to_all | solution.py:85
  205.5 5.5 %multiply_convert_fusion.2 = (bf16[8,640,512]{2,1,0:T(8,128)(2,1)}, f32[8,640,512]{2,1,0:T(8,128)S(1)}) fusion(f32[512]{0:T(512)S(1)} %copy-done.8, bf16[8,192,640]{2,1,0:T(8,128)(2,1)S(1)} %bitcast.104, bf16[192,512]{1,0:T(8,128)(2,1)S(1)} %copy-done), kind=kOutput, calls=%fused_computation.22 | convolution fusion | flops 1032847360 | bytes 17893376 | tf_op jit(solution)/shard_map/lkc,kh->lch/dot_general | solution.py:87
  211.0 8.7 %convert_reduce_fusion = (f32[512]{0:T(512)S(1)}, bf16[8,640,512]{2,1,0:T(8,128)(2,1)S(1)}) fusion(f32[8,640,512]{2,1,0:T(8,128)S(1)} %get-tuple-element.25, f32[512]{0:T(512)S(1)} %copy-done.8, bf16[8,192,640]{2,1,0:T(8,128)(2,1)S(1)} %copy-done.3, bf16[512,192]{0,1:T(8,128)(2,1)S(1)} %copy-done.7), kind=kOutput, calls=%fused_computation.21 | convolution fusion | flops 1066925568 | bytes 17895424 | tf_op jit(solution)/shard_map/lkc,hk->lch/dot_general | solution.py:99
  222.7 26.9 %all_to_all.69 = bf16[8,192,640]{2,0,1:T(8,128)(2,1)S(1)} all-to-all(bf16[8,192,640]{2,0,1:T(8,128)(2,1)S(1)} %copy.33), channel_id=1, replica_groups=mesh['lat'=8,'lon'=4] {'lon'}, dimensions={1} | all-to-all | bytes 3932160 | tf_op jit(solution)/shard_map/all_to_all | solution.py:128
  253.4 9.0 %fusion.14 = bf16[1280,8,48,2]{0,2,3,1:T(8,128)(2,1)S(1)} fusion(bf16[1280,1,2560]{2,0,1:T(8,128)(2,1)} %get-tuple-element.28, bf16[1280,1,2560]{2,0,1:T(8,128)(2,1)} %get-tuple-element.29, bf16[8,48,2560,1]{2,1,0,3:T(8,128)(2,1)} %reshape.462), kind=kOutput, calls=%fused_computation.31 | convolution fusion | flops 5060362240 | bytes 17039360 | tf_op jit(solution)/shard_map/gcn,lkn->glkc/dot_general | solution.py:129
  265.2 6.4 %all_to_all.61 = bf16[8,160,768]{1,0,2:T(8,128)(2,1)S(1)} reshape(bf16[1280,8,48,2]{0,3,2,1:T(2,128)(2,1)} %copy.35) | data formatting | bytes 3932160 | tf_op jit(solution)/shard_map/all_to_all | solution.py:133
  271.6 3.2 copy.36
  274.8 5.7 %all-to-all-start.3 = ((bf16[8,160,768]{2,1,0:T(8,128)(2,1)}), bf16[8,160,768]{2,1,0:T(8,128)(2,1)S(1)}, u32[]{:S(2)}, u32[]{:S(2)}) async-start(bf16[8,160,768]{2,1,0:T(8,128)(2,1)} %copy.36), calls=%async_computation.3 | async-start | bytes 3932160 | tf_op jit(solution)/shard_map/all_to_all | solution.py:133
  282.9 4.6 convolution_bitcast_fusion.1
  289.8 5.6 %fusion.23 = bf16[8,192,640]{2,1,0:T(8,128)(2,1)} fusion(f32[192]{0:T(256)S(1)} %copy-done.9, bf16[8,640,512]{2,1,0:T(8,128)(2,1)} %get-tuple-element.24, bf16[512,192]{0,1:T(8,128)(2,1)S(1)} %copy-done.7), kind=kOutput, calls=%fused_computation.41 | convolution fusion | flops 1008599040 | bytes 7406336 | tf_op jit(solution)/shard_map/lch,hk->lkc/dot_general | solution.py:92
  295.4 136.8 %all-reduce.3.cloned.1.call-done = f32[386,512]{1,0:T(8,128)} async-done(((f32[386,512]{1,0:T(8,128)}), f32[386,512]{1,0:T(8,128)}) %all-reduce.3.cloned.1.call-update) | async-done | bytes 790544 | tf_op jit(solution)/shard_map/psum | solution.py:123
  439.1 4.6 reshape.456
  446.1 3.4 rev.8
  449.5 20.5 %bitcast_convert_fusion = bf16[80,96,1408]{2,1,0:T(8,128)(2,1)} fusion(bf16[80,1,64,1408]{3,2,1,0:T(8,128)(2,1)} %get-tuple-element.7, bf16[80,1,64,1408]{3,2,1,0:T(8,128)(2,1)} %get-tuple-element.6, bf16[80,2,32,96]{3,2,1,0:T(8,128)(2,1)S(1)} %rev.8, bf16[80,2,32,96]{3,2,1,0:T(8,128)(2,1)} %get-tuple-element.8), kind=kOutput, calls=%fused_computation | convolution fusion | flops 2797404160 | bytes 52428800 | tf_op jit(solution)/shard_map/pqlk,pqlj->pkj/dot_general | solution.py:138
  (63 shorter events, 35.4 us)
Async XLA Ops:
  7.2 198.3 %copy-start = (bf16[192,512]{1,0:T(8,128)(2,1)S(1)}, bf16[192,512]{1,0:T(8,128)(2,1)}, u32[]{:S(2)}) copy-start(bf16[192,512]{1,0:T(8,128)(2,1)} %param.11) | copy-start | bytes 589828
  8.3 7.3 %slice-start = ((s8[7208960]{0:T(1024)(128)(4,1)}), s8[4194304]{0:T(1024)(128)(4,1)S(1)}, s32[]{:S(2)}) async-start(s8[7208960]{0:T(1024)(128)(4,1)} %bitcast.95), calls=%async_computation.5 | async-start | bytes 8388608
  8.6 7.1 %slice-start.1 = ((s8[7208960]{0:T(1024)(128)(4,1)}), s8[3014656]{0:T(1024)(128)(4,1)S(1)}, s32[]{:S(2)}) async-start(s8[7208960]{0:T(1024)(128)(4,1)} %bitcast.95), calls=%async_computation.6 | async-start | bytes 6029312
  58.3 13.3 %copy-start.6 = (s32[640]{0:T(1024)S(1)}, s32[640]{0:T(1024)}, u32[]{:S(2)}) copy-start(s32[640]{0:T(1024)} %param.8) | copy-start | bytes 7684
  64.6 66.8 %all-to-all-start = ((bf16[160,8,768]{2,0,1:T(8,128)(2,1)}), bf16[160,8,768]{2,0,1:T(8,128)(2,1)S(1)}, u32[]{:S(2)}, u32[]{:S(2)}) async-start(bf16[160,8,768]{2,0,1:T(8,128)(2,1)} %copy.25), calls=%async_computation | async-start | bytes 3932160 | tf_op jit(solution)/shard_map/all_to_all | solution.py:77
  131.5 1.3 copy-start.1
  192.7 12.8 %copy-start.8 = (f32[512]{0:T(512)S(1)}, f32[512]{0:T(512)}, u32[]{:S(2)}) copy-start(f32[512]{0:T(512)} %param.12) | copy-start | bytes 6148
  205.5 5.6 %copy-start.5 = (bf16[8,48,4,640]{3,1,2,0:T(8,128)(2,1)}, bf16[8,48,4,640]{3,1,2,0:T(8,128)(2,1)S(1)}, u32[]{:S(2)}) copy-start(bf16[8,48,4,640]{3,1,2,0:T(8,128)(2,1)S(1)} %copy.32) | copy-start | bytes 5898244
  205.5 5.5 %copy-start.3 = (bf16[8,192,640]{2,1,0:T(8,128)(2,1)S(1)}, bf16[8,192,640]{2,1,0:T(8,128)(2,1)}, u32[]{:S(2)}) copy-start(bf16[8,192,640]{2,1,0:T(8,128)(2,1)} %param.15) | copy-start | bytes 5898244
  205.5 5.5 %copy-start.7 = (bf16[512,192]{0,1:T(8,128)(2,1)S(1)}, bf16[512,192]{0,1:T(8,128)(2,1)}, u32[]{:S(2)}) copy-start(bf16[512,192]{0,1:T(8,128)(2,1)} %param.13) | copy-start | bytes 589828
  219.7 29.9 %copy-start.2 = (bf16[8,640,512]{2,1,0:T(8,128)(2,1)}, bf16[8,640,512]{2,1,0:T(8,128)(2,1)S(1)}, u32[]{:S(2)}) copy-start(bf16[8,640,512]{2,1,0:T(8,128)(2,1)S(1)} %get-tuple-element.27) | copy-start | bytes 15728644
  274.8 161.9 %all-to-all-start.3 = ((bf16[8,160,768]{2,1,0:T(8,128)(2,1)}), bf16[8,160,768]{2,1,0:T(8,128)(2,1)S(1)}, u32[]{:S(2)}, u32[]{:S(2)}) async-start(bf16[8,160,768]{2,1,0:T(8,128)(2,1)} %copy.36), calls=%async_computation.3 | async-start | bytes 3932160 | tf_op jit(solution)/shard_map/all_to_all | solution.py:133
  280.6 151.6 %all-reduce.3.cloned.1.call-start = ((), (), s32[]{:S(2)}) async-start(), calls=%async_computation.4 | async-start | bytes 1605632 | tf_op jit(solution)/shard_map/psum | solution.py:123
  280.9 6.7 %copy-start.4 = (bf16[8,192,640]{2,1,0:T(8,128)(2,1)S(1)}, bf16[8,192,640]{2,1,0:T(8,128)(2,1)}, u32[]{:S(2)}) copy-start(bf16[8,192,640]{2,1,0:T(8,128)(2,1)} %param.15) | copy-start | bytes 5898244
  280.9 6.7 %slice-start.2 = ((s8[5242880]{0:T(1024)(128)(4,1)}), s8[4194304]{0:T(1024)(128)(4,1)S(1)}, s32[]{:S(2)}) async-start(s8[5242880]{0:T(1024)(128)(4,1)} %bitcast.110), calls=%async_computation.7 | async-start | bytes 8388608
  282.9 4.6 slice-start.3
  287.5 2.3 copy-start.9
Sparse Core Ops, SparseCore 0:
  289.9 142.2 all-reduce.2
where the time goes:
time: 484 us; the launch traced here: 477 us
  waiting for transfers between devices  137 us (28%)
  local copies, waits for them, and re-layouts  113 us (23%)
  matrix products  85.8 us (18%)
  other arithmetic  59.6 us (12%)
  blocking collectives  54.4 us (11%)
  between operations  14.7 us (3%)
  starting transfers between devices  12.9 us (3%)
    psum x1, waiting for transfers between devices, per_device(): summed = lax.psum(stacked, ('lat', 'lon'))  137 us
    all_to_all x1, blocking collectives, per_device(): lax.all_to_all(all_columns, 'lon', split_axis=2, concat_axis=1, tiled=True)  27.4 us
    all_to_all x1, blocking collectives, per_device(): lax.all_to_all(grid_grad, 'lon', split_axis=1, concat_axis=2, tiled=True)  26.9 us
    dot_general x1, matrix products, per_device(): jnp.einsum('pqlk,pqlj->pkj', pair_grad, basis, preferred_element_type=jnp...  20.5 us
    dot_general x1, matrix products, per_device(): jnp.einsum('pqlj,pkj->pqlk', basis, spectral, preferred_element_type=jnp....  20 us
    unnamed x30, local copies, waits for them, and re-layouts  17.3 us
    select_n x1, other arithmetic, per_device(): jnp.where(lower_part[:, None, :], rows, zero)  14.2 us
    add x1, local copies, waits for them, and re-layouts, fourier_table(): sin_a[:, :, None] * cos_b[:, None, :]  14 us
  transfers between devices with their start and end apart: 3, of which 1 were waited for; matrix products, arithmetic and copies ran while one was open for 17% of the time, Pallas kernels for 0%

commit v1 on v0

--- a/solution.py
+++ b/solution.py
@@ -120,7 +120,9 @@
         ],
         axis=0,
     )
-    summed = lax.psum(stacked, ("lat", "lon"))
+    summed = stacked
+    for q in ("lon", "lat"):
+        summed = lax.psum(summed, q)
     in_weight_grad = summed[:channels, :hid]
     out_weight_grad = summed[channels : 2 * channels, :hid].T
     in_bias_grad = summed[2 * channels, :hid]

time: 484 us -> 457 us (0.944)
  waiting for transfers between devices: 137 us -> 107 us
    psum x1 -> x2, waiting for transfers between devices: 137 us -> 107 us  [per_device(): summed = lax.psum(summed, q)]
  transfers between devices with their start and end apart: 3 -> 4, of which waited for: 1 -> 2; matrix products, arithmetic and copies ran while one was open for 17% -> 18% of each run, Pallas kernels for 0% -> 0%
where the time goes in v1:
time: 457 us; the launch traced here: 448 us
  local copies, waits for them, and re-layouts  113 us (25%)
  waiting for transfers between devices  107 us (23%)
  matrix products  85.8 us (19%)
  other arithmetic  59.6 us (13%)
  blocking collectives  54.4 us (12%)
  between operations  14.7 us (3%)
  starting transfers between devices  13 us (3%)
    psum x2, waiting for transfers between devices, per_device(): summed = lax.psum(summed, q)  107 us
    all_to_all x1, blocking collectives, per_device(): lax.all_to_all(all_columns, 'lon', split_axis=2, concat_axis=1, tiled=True)  27.4 us
    all_to_all x1, blocking collectives, per_device(): lax.all_to_all(grid_grad, 'lon', split_axis=1, concat_axis=2, tiled=True)  26.9 us
    dot_general x1, matrix products, per_device(): jnp.einsum('pqlk,pqlj->pkj', pair_grad, basis, preferred_element_type=jnp...  20.5 us
    dot_general x1, matrix products, per_device(): jnp.einsum('pqlj,pkj->pqlk', basis, spectral, preferred_element_type=jnp....  20 us
    unnamed x30, local copies, waits for them, and re-layouts  17.3 us
    select_n x1, other arithmetic, per_device(): jnp.where(lower_part[:, None, :], rows, zero)  14.2 us
    add x1, local copies, waits for them, and re-layouts, fourier_table(): sin_a[:, :, None] * cos_b[:, None, :]  14 us
  transfers between devices with their start and end apart: 4, of which 2 were waited for; matrix products, arithmetic and copies ran while one was open for 18% of the time, Pallas kernels for 0%

profile of v1, /device:TPU:1, one launch (start us, length us, event | category | flops | bytes accessed | tf_op | source)
XLA Modules:
  0.0 447.8 jit_solution(9319112335756062495)
XLA Ops:
  8.6 7.1 %multiply_bitcast_fusion = bf16[80,1,32,1408]{3,2,1,0:T(8,128)(2,1)} fusion(bf16[80,32,1408]{2,1,0:T(8,128)(2,1)} %param.10, bf16[80,1408]{1,0:T(8,128)(2,1)S(1)} %select_convert_fusion), kind=kLoop, calls=%fused_computation.25 | loop fusion | flops 3604480 | bytes 14643200 | tf_op jit(solution)/shard_map/concatenate | solution.py:60
  15.7 14.2 %broadcast_select_fusion.1 = (bf16[80,1,64,1408]{3,2,1,0:T(8,128)(2,1)}, bf16[80,1,64,1408]{3,2,1,0:T(8,128)(2,1)}) fusion(pred[80,1408]{1,0:T(8,128)(4,1)S(1)} %get-tuple-element.22, bf16[80,1,32,1408]{3,2,1,0:T(8,128)(2,1)} %multiply_bitcast_fusion, bf16[80,1,32,1408]{3,2,1,0:T(8,128)(2,1)S(1)} %bitcast.97, pred[80,1408]{1,0:T(8,128)(4,1)S(1)} %get-tuple-element.23), kind=kLoop, calls=%fused_computation.8 | loop fusion | flops 43253760 | bytes 43479040 | tf_op jit(solution)/shard_map/jit(_where)/select_n | solution.py:64
  29.8 20.0 %fusion.18 = bf16[80,2,64,96]{3,2,1,0:T(8,128)(2,1)} fusion(bf16[80,96,1408]{2,1,0:T(8,128)(2,1)} %param.9, bf16[80,1,64,1408]{3,2,1,0:T(8,128)(2,1)} %get-tuple-element.7, bf16[80,1,64,1408]{3,2,1,0:T(8,128)(2,1)} %get-tuple-element.6), kind=kOutput, calls=%fused_computation.36 | convolution fusion | flops 2783641600 | bytes 52428800 | tf_op jit(solution)/shard_map/pqlj,pkj->pqlk/dot_general | solution.py:70
  49.8 3.4 fusion.52
  61.4 3.2 copy.25
  64.6 6.9 %all-to-all-start = ((bf16[160,8,768]{2,0,1:T(8,128)(2,1)}), bf16[160,8,768]{2,0,1:T(8,128)(2,1)S(1)}, u32[]{:S(2)}, u32[]{:S(2)}) async-start(bf16[160,8,768]{2,0,1:T(8,128)(2,1)} %copy.25), calls=%async_computation | async-start | bytes 3932160 | tf_op jit(solution)/shard_map/all_to_all | solution.py:77
  75.9 13.6 %multiply_subtract_fusion = (f32[1280,20,128]{0,2,1:T(8,128)}, f32[1280,20,128]{0,2,1:T(8,128)}) fusion(f32[1280,128]{0,1:T(8,128)S(1)} %get-tuple-element.21, f32[1280,20]{0,1:T(8,128)} %get-tuple-element.17, f32[1280,128]{0,1:T(8,128)S(1)} %get-tuple-element.20, f32[1280,20]{0,1:T(8,128)} %get-tuple-element.16), kind=kLoop, calls=%fused_computation.13 | loop fusion | flops 19660800 | bytes 27729920 | tf_op jit(solution)/shard_map/sub | solution.py:38
  89.6 14.0 %copy.29 = f32[1280,1,2560]{2,0,1:T(8,128)} copy(f32[1280,1,2560]{0,2,1:T(8,128)} %bitcast.94) | data formatting | bytes 26214400 | tf_op jit(solution)/shard_map/add | solution.py:39
  103.6 14.0 %copy.28 = f32[1280,1,2560]{2,0,1:T(8,128)} copy(f32[1280,1,2560]{0,2,1:T(8,128)} %bitcast.93) | data formatting | bytes 26214400 | tf_op jit(solution)/shard_map/sub | solution.py:38
  117.5 13.9 %multiply_convert_fusion = (bf16[1280,1,2560]{2,0,1:T(8,128)(2,1)}, bf16[1280,1,2560]{2,0,1:T(8,128)(2,1)}) fusion(f32[1280,1,2560]{2,0,1:T(8,128)} %copy.29, f32[1280]{0:T(1024)S(1)} %get-tuple-element.19, f32[1280,1,2560]{2,0,1:T(8,128)} %copy.28, f32[1280]{0:T(1024)S(1)} %get-tuple-element.18), kind=kLoop, calls=%fused_computation.10 | loop fusion | flops 13107200 | bytes 39331840 | tf_op jit(solution)/shard_map/convert.1
  132.7 4.1 copy.26
  136.8 5.2 %reshape.454 = bf16[1280,8,48,2]{0,3,2,1:T(2,128)(2,1)} reshape(bf16[8,160,768]{1,0,2:T(8,128)(2,1)S(1)} %copy.26) | data formatting | bytes 3932160 | tf_op jit(solution)/shard_map/reshape | solution.py:79
  142.1 8.9 %fusion.12 = bf16[8,48,2560]{2,1,0:T(8,128)(2,1)S(1)} fusion(bf16[1280,1,2560]{2,0,1:T(8,128)(2,1)} %get-tuple-element.28, bf16[1280,1,2560]{2,0,1:T(8,128)(2,1)} %get-tuple-element.29, bf16[1280,8,48,2]{0,3,2,1:T(2,128)(2,1)} %reshape.454), kind=kOutput, calls=%fused_computation.27 | convolution fusion | flops 5040701440 | bytes 17039360 | tf_op jit(solution)/shard_map/glkc,gcn->lkn/dot_general | solution.py:82
  151.0 5.4 %copy.31 = bf16[8,48,2560]{1,0,2:T(8,128)(2,1)} copy(bf16[8,48,2560]{2,1,0:T(8,128)(2,1)S(1)} %fusion.12) | data formatting | bytes 3932160 | tf_op jit(solution)/shard_map/convert_element_type | solution.py:84
  156.4 8.8 %reshape.467 = bf16[4,2,122880]{2,1,0:T(2,128)(2,1)S(1)} reshape(bf16[2560,8,48]{2,1,0:T(8,128)(2,1)} %bitcast.98) | data formatting | bytes 3932160
  165.3 27.4 %all_to_all.68 = bf16[4,2,122880]{2,1,0:T(2,128)(2,1)} all-to-all(bf16[4,2,122880]{2,1,0:T(2,128)(2,1)S(1)} %reshape.467), channel_id=1, replica_groups=mesh['lat'=8,'lon'=4] {'lon'}, dimensions={0} | all-to-all | bytes 3932160 | tf_op jit(solution)/shard_map/all_to_all | solution.py:85
  192.7 7.1 %reshape.468 = bf16[2560,8,48]{2,1,0:T(8,128)(2,1)} reshape(bf16[4,2,122880]{2,1,0:T(2,128)(2,1)} %all_to_all.68) | data formatting | bytes 3932160
  199.8 5.7 %copy.32 = bf16[8,48,4,640]{3,1,2,0:T(8,128)(2,1)S(1)} copy(bf16[8,48,4,640]{1,0,3,2:T(8,128)(2,1)} %bitcast.99) | data formatting | bytes 3932160 | tf_op jit(solution)/shard_map/all_to_all | solution.py:85
  205.5 5.5 %multiply_convert_fusion.2 = (bf16[8,640,512]{2,1,0:T(8,128)(2,1)}, f32[8,640,512]{2,1,0:T(8,128)S(1)}) fusion(f32[512]{0:T(512)S(1)} %copy-done.8, bf16[8,192,640]{2,1,0:T(8,128)(2,1)S(1)} %bitcast.104, bf16[192,512]{1,0:T(8,128)(2,1)S(1)} %copy-done), kind=kOutput, calls=%fused_computation.22 | convolution fusion | flops 1032847360 | bytes 17893376 | tf_op jit(solution)/shard_map/lkc,kh->lch/dot_general | solution.py:87
  211.0 8.7 %convert_reduce_fusion = (f32[512]{0:T(512)S(1)}, bf16[8,640,512]{2,1,0:T(8,128)(2,1)S(1)}) fusion(f32[8,640,512]{2,1,0:T(8,128)S(1)} %get-tuple-element.25, f32[512]{0:T(512)S(1)} %copy-done.8, bf16[8,192,640]{2,1,0:T(8,128)(2,1)S(1)} %copy-done.3, bf16[512,192]{0,1:T(8,128)(2,1)S(1)} %copy-done.7), kind=kOutput, calls=%fused_computation.21 | convolution fusion | flops 1066925568 | bytes 17895424 | tf_op jit(solution)/shard_map/lkc,hk->lch/dot_general | solution.py:99
  222.7 26.9 %all_to_all.69 = bf16[8,192,640]{2,0,1:T(8,128)(2,1)S(1)} all-to-all(bf16[8,192,640]{2,0,1:T(8,128)(2,1)S(1)} %copy.33), channel_id=1, replica_groups=mesh['lat'=8,'lon'=4] {'lon'}, dimensions={1} | all-to-all | bytes 3932160 | tf_op jit(solution)/shard_map/all_to_all | solution.py:130
  253.4 9.0 %fusion.14 = bf16[1280,8,48,2]{0,2,3,1:T(8,128)(2,1)S(1)} fusion(bf16[1280,1,2560]{2,0,1:T(8,128)(2,1)} %get-tuple-element.28, bf16[1280,1,2560]{2,0,1:T(8,128)(2,1)} %get-tuple-element.29, bf16[8,48,2560,1]{2,1,0,3:T(8,128)(2,1)} %reshape.462), kind=kOutput, calls=%fused_computation.31 | convolution fusion | flops 5060362240 | bytes 17039360 | tf_op jit(solution)/shard_map/gcn,lkn->glkc/dot_general | solution.py:131
  265.2 6.4 %all_to_all.61 = bf16[8,160,768]{1,0,2:T(8,128)(2,1)S(1)} reshape(bf16[1280,8,48,2]{0,3,2,1:T(2,128)(2,1)} %copy.35) | data formatting | bytes 3932160 | tf_op jit(solution)/shard_map/all_to_all | solution.py:135
  271.6 3.2 copy.36
  274.8 5.7 %all-to-all-start.3 = ((bf16[8,160,768]{2,1,0:T(8,128)(2,1)}), bf16[8,160,768]{2,1,0:T(8,128)(2,1)S(1)}, u32[]{:S(2)}, u32[]{:S(2)}) async-start(bf16[8,160,768]{2,1,0:T(8,128)(2,1)} %copy.36), calls=%async_computation.3 | async-start | bytes 3932160 | tf_op jit(solution)/shard_map/all_to_all | solution.py:135
  282.7 4.6 %convolution_bitcast_fusion.1 = f32[192,512]{1,0:T(8,128)S(1)} fusion(bf16[8,192,640]{2,1,0:T(8,128)(2,1)} %bitcast.105, bf16[8,640,512]{2,1,0:T(8,128)(2,1)} %copy-done.2), kind=kOutput, calls=%fused_computation.43 | convolution fusion | flops 1006632960 | bytes 7602176 | tf_op jit(solution)/shard_map/lkc,lch->kh/dot_general | solution.py:103
  289.8 34.5 %all-reduce.4.cloned.1.call-done = f32[386,512]{1,0:T(8,128)} async-done(((f32[386,512]{1,0:T(8,128)}), f32[386,512]{1,0:T(8,128)}) %all-reduce.4.cloned.1.call-update) | async-done | bytes 790544 | tf_op jit(solution)/shard_map/psum | solution.py:125
  324.4 5.6 %fusion.23 = bf16[8,192,640]{2,1,0:T(8,128)(2,1)} fusion(f32[192]{0:T(256)S(1)} %copy-done.9, bf16[8,640,512]{2,1,0:T(8,128)(2,1)} %get-tuple-element.24, bf16[512,192]{0,1:T(8,128)(2,1)S(1)} %copy-done.7), kind=kOutput, calls=%fused_computation.41 | convolution fusion | flops 1008599040 | bytes 7406336 | tf_op jit(solution)/shard_map/lch,hk->lkc/dot_general | solution.py:92
  330.0 72.9 %all-reduce.6.cloned.1.call-done = f32[386,512]{1,0:T(8,128)} async-done(((f32[386,512]{1,0:T(8,128)}), f32[386,512]{1,0:T(8,128)}) %all-reduce.6.cloned.1.call-update) | async-done | bytes 790544 | tf_op jit(solution)/shard_map/psum | solution.py:125
  409.9 4.6 %reshape.456 = bf16[80,2,64,96]{3,2,1,0:T(8,128)(2,1)S(1)} reshape(bf16[160,8,768]{2,1,0:T(8,128)(2,1)} %copy.37) | data formatting | bytes 3932160 | tf_op jit(solution)/shard_map/reshape | solution.py:136
  416.8 3.4 rev.8
  420.2 20.5 %bitcast_convert_fusion = bf16[80,96,1408]{2,1,0:T(8,128)(2,1)} fusion(bf16[80,1,64,1408]{3,2,1,0:T(8,128)(2,1)} %get-tuple-element.7, bf16[80,1,64,1408]{3,2,1,0:T(8,128)(2,1)} %get-tuple-element.6, bf16[80,2,32,96]{3,2,1,0:T(8,128)(2,1)S(1)} %rev.8, bf16[80,2,32,96]{3,2,1,0:T(8,128)(2,1)} %get-tuple-element.8), kind=kOutput, calls=%fused_computation | convolution fusion | flops 2797404160 | bytes 52428800 | tf_op jit(solution)/shard_map/pqlk,pqlj->pkj/dot_general | solution.py:140
  (66 shorter events, 38.6 us)
Async XLA Ops:
  7.2 198.3 %copy-start = (bf16[192,512]{1,0:T(8,128)(2,1)S(1)}, bf16[192,512]{1,0:T(8,128)(2,1)}, u32[]{:S(2)}) copy-start(bf16[192,512]{1,0:T(8,128)(2,1)} %param.11) | copy-start | bytes 589828
  8.3 7.3 %slice-start = ((s8[7208960]{0:T(1024)(128)(4,1)}), s8[4194304]{0:T(1024)(128)(4,1)S(1)}, s32[]{:S(2)}) async-start(s8[7208960]{0:T(1024)(128)(4,1)} %bitcast.95), calls=%async_computation.6 | async-start | bytes 8388608
  8.6 7.1 %slice-start.1 = ((s8[7208960]{0:T(1024)(128)(4,1)}), s8[3014656]{0:T(1024)(128)(4,1)S(1)}, s32[]{:S(2)}) async-start(s8[7208960]{0:T(1024)(128)(4,1)} %bitcast.95), calls=%async_computation.7 | async-start | bytes 6029312
  58.3 13.3 %copy-start.6 = (s32[640]{0:T(1024)S(1)}, s32[640]{0:T(1024)}, u32[]{:S(2)}) copy-start(s32[640]{0:T(1024)} %param.8) | copy-start | bytes 7684
  64.6 66.8 %all-to-all-start = ((bf16[160,8,768]{2,0,1:T(8,128)(2,1)}), bf16[160,8,768]{2,0,1:T(8,128)(2,1)S(1)}, u32[]{:S(2)}, u32[]{:S(2)}) async-start(bf16[160,8,768]{2,0,1:T(8,128)(2,1)} %copy.25), calls=%async_computation | async-start | bytes 3932160 | tf_op jit(solution)/shard_map/all_to_all | solution.py:77
  131.5 1.3 copy-start.1
  192.7 12.8 %copy-start.8 = (f32[512]{0:T(512)S(1)}, f32[512]{0:T(512)}, u32[]{:S(2)}) copy-start(f32[512]{0:T(512)} %param.12) | copy-start | bytes 6148
  205.5 5.6 %copy-start.5 = (bf16[8,48,4,640]{3,1,2,0:T(8,128)(2,1)}, bf16[8,48,4,640]{3,1,2,0:T(8,128)(2,1)S(1)}, u32[]{:S(2)}) copy-start(bf16[8,48,4,640]{3,1,2,0:T(8,128)(2,1)S(1)} %copy.32) | copy-start | bytes 5898244
  205.5 5.5 %copy-start.3 = (bf16[8,192,640]{2,1,0:T(8,128)(2,1)S(1)}, bf16[8,192,640]{2,1,0:T(8,128)(2,1)}, u32[]{:S(2)}) copy-start(bf16[8,192,640]{2,1,0:T(8,128)(2,1)} %param.15) | copy-start | bytes 5898244
  205.5 5.5 %copy-start.7 = (bf16[512,192]{0,1:T(8,128)(2,1)S(1)}, bf16[512,192]{0,1:T(8,128)(2,1)}, u32[]{:S(2)}) copy-start(bf16[512,192]{0,1:T(8,128)(2,1)} %param.13) | copy-start | bytes 589828
  219.7 29.9 %copy-start.2 = (bf16[8,640,512]{2,1,0:T(8,128)(2,1)}, bf16[8,640,512]{2,1,0:T(8,128)(2,1)S(1)}, u32[]{:S(2)}) copy-start(bf16[8,640,512]{2,1,0:T(8,128)(2,1)S(1)} %get-tuple-element.27) | copy-start | bytes 15728644
  274.8 132.7 %all-to-all-start.3 = ((bf16[8,160,768]{2,1,0:T(8,128)(2,1)}), bf16[8,160,768]{2,1,0:T(8,128)(2,1)S(1)}, u32[]{:S(2)}, u32[]{:S(2)}) async-start(bf16[8,160,768]{2,1,0:T(8,128)(2,1)} %copy.36), calls=%async_computation.3 | async-start | bytes 3932160 | tf_op jit(solution)/shard_map/all_to_all | solution.py:135
  280.6 43.8 %all-reduce.4.cloned.1.call-start = ((), (), s32[]{:S(2)}) async-start(), calls=%async_computation.4 | async-start | bytes 1605632 | tf_op jit(solution)/shard_map/psum | solution.py:125
  280.6 6.7 %copy-start.4 = (bf16[8,192,640]{2,1,0:T(8,128)(2,1)S(1)}, bf16[8,192,640]{2,1,0:T(8,128)(2,1)}, u32[]{:S(2)}) copy-start(bf16[8,192,640]{2,1,0:T(8,128)(2,1)} %param.15) | copy-start | bytes 5898244
  280.6 6.7 %slice-start.2 = ((s8[5242880]{0:T(1024)(128)(4,1)}), s8[4194304]{0:T(1024)(128)(4,1)S(1)}, s32[]{:S(2)}) async-start(s8[5242880]{0:T(1024)(128)(4,1)} %bitcast.110), calls=%async_computation.8 | async-start | bytes 8388608
  282.7 4.6 %slice-start.3 = ((s8[5242880]{0:T(1024)(128)(4,1)}), s8[1048576]{0:T(1024)(128)(4,1)S(1)}, s32[]{:S(2)}) async-start(s8[5242880]{0:T(1024)(128)(4,1)} %bitcast.110), calls=%async_computation.9 | async-start | bytes 2097152
  287.3 37.1 %copy-start.9 = (f32[192]{0:T(256)S(1)}, f32[192]{0:T(256)}, u32[]{:S(2)}) copy-start(f32[192]{0:T(256)} %param.14) | copy-start | bytes 2308
  289.5 113.4 %all-reduce.6.cloned.1.call-start = ((), (), s32[]{:S(2)}) async-start(), calls=%async_computation.5 | async-start | bytes 1605632 | tf_op jit(solution)/shard_map/psum | solution.py:125
Sparse Core Ops, SparseCore 0:
  289.6 34.6 all-reduce.3
  327.8 75.0 all-reduce.5
